TPU v7x, 32 devices: a whole 2x2x4 slice. The times are simulated.
32 devices in a mesh: runs: 2 (over y), row: 4 (over z), col: 2 (over x), sub: 2 (over core).
Axes of the slice: x: 2, y: 2, z: 4, core: 2. Of those that a mesh axis runs over, the one named last changes fastest.
Arguments:
- packed: bfloat16 [4, 2048, 256], P(('col', 'sub'), ('runs', 'row')), parts along dimension 1, may hold values from -6 to 6
- h_real: bfloat16 [8, 4, 128, 128], P('row'), may hold values from -0.25 to 0.25
- h_imag: bfloat16 [8, 4, 128, 128], P('row'), may hold values from -0.25 to 0.25
- h_cols: int32 [8, 4], P('row'), may hold values from 0 to 7, as said below
Outputs:
- evolved: float32 [4, 2048, 256], P(('col', 'sub'), ('runs', 'row')), parts along dimension 1
There are 2 independent parts, one for each index of `runs`. A program takes and returns all parts, laid end to end along the dimension named above; an argument that names none is the same for every part. Nothing has to cross between parts.
Inputs may be any that keep to these rules, and one draw needn't show every extreme that they name: h_cols[b, 0] = b, and h_cols[b, 1], h_cols[b, 2], h_cols[b, 3] are (b + e) mod 8 for three different e among -2, -1, 1, 2.
All inputs are finite; a program needn't handle non-finite values.
Results may differ from a plain program's by a relative error of at most 0.0027.
Values may be sent and summed in bfloat16 or wider, within the bound.
A program may use at most 64 MiB of HBM per device.

v0:
```python
import functools

import jax
import jax.numpy as jnp
from jax import lax
from jax.experimental import pallas as pl
from jax.experimental.pallas import tpu as pltpu
from jax.sharding import PartitionSpec as P

TERMS = 3


step_size = 0.5


def extended(block, sides, width):
    for axis, dim in sides:
        count = lax.axis_size(axis)
        forward = [(i, i + 1) for i in range(count - 1)]
        forward.append((count - 1, 0))
        backward = [(target, source) for source, target in forward]
        low = lax.ppermute(
            lax.slice_in_dim(block, block.shape[dim] - width, None, axis=dim), axis, forward
        )
        high = lax.ppermute(lax.slice_in_dim(block, 0, width, axis=dim), axis, backward)
        block = jnp.concatenate([low, block, high], axis=dim)
    return block


def mirror(stacked):
    groups, rows_here, col_count = stacked.shape
    piece_count = lax.axis_size(("col", "sub"))
    band_count = lax.axis_size("row")
    piece_len = rows_here // piece_count
    split_rows = stacked.reshape(groups, piece_count, piece_len, col_count)
    arrived = lax.all_to_all(split_rows, ("col", "sub"), split_axis=1, concat_axis=1, tiled=True)
    turned = jnp.swapaxes(arrived.reshape(groups, rows_here, col_count), 1, 2).reshape(
        groups, band_count, piece_len, rows_here
    )
    landed = lax.all_to_all(turned, "row", split_axis=1, concat_axis=1, tiled=True)
    spread = landed.reshape(groups, band_count, piece_len, piece_count, piece_len)
    placed = jnp.transpose(spread, (0, 3, 2, 1, 4))
    return placed.reshape(groups, rows_here, col_count)


def body(packed, h_real, h_imag, h_cols):
    packed_here = packed.reshape(packed.shape[1], packed.shape[2])
    rows_here, col_count = packed_here.shape
    band_index = lax.axis_index("row")
    piece_index = lax.axis_index(("col", "sub"))
    piece_len = rows_here // lax.axis_size(("col", "sub"))
    flipped = mirror(packed_here[None])[0]
    row_ids = band_index * rows_here + jnp.arange(rows_here, dtype=jnp.int32)[:, None]
    col_local = jnp.arange(col_count, dtype=jnp.int32)[None, :]
    col_ids = col_local // piece_len * rows_here + piece_index * piece_len + col_local % piece_len
    upper_mask = row_ids <= col_ids
    real_part = jnp.where(upper_mask, packed_here, flipped)
    imag_part = jnp.where(
        row_ids > col_ids,
        packed_here,
        jnp.where(row_ids < col_ids, -flipped, jnp.zeros_like(flipped)),
    )
    current = jnp.stack([real_part, imag_part])
    summed = current.astype(jnp.float32)
    combined = jnp.stack([jnp.stack([h_imag, h_real], 2), jnp.stack([-h_real, h_imag], 2)])
    local_blocks = h_real.shape[0]
    block_len = h_real.shape[2]
    block_total = lax.axis_size("row") * local_blocks
    block_ids = band_index * local_blocks + jnp.arange(local_blocks, dtype=jnp.int32)[:, None]
    offsets = (h_cols - block_ids + 2) % block_total - 2
    starts = (
        (jnp.arange(local_blocks, dtype=jnp.int32)[:, None] + offsets + 2) * block_len
    ).reshape(-1)
    for term_index in range(1, TERMS + 1):
        padded = extended(current, (("row", 1),), 2 * block_len)
        sliced = jax.vmap(
            lambda row_start: lax.dynamic_slice_in_dim(padded, row_start, block_len, 1)
        )(starts)
        gathered = sliced.reshape(local_blocks, 4, 2, block_len, col_count)
        product = jnp.einsum(
            "obsgij,bsgjc->obic", combined, gathered, preferred_element_type=jnp.float32
        )
        generator = product.reshape(2, rows_here, col_count).astype(jnp.bfloat16)
        mirror_part = mirror(generator).astype(jnp.float32)
        own_part = generator.astype(jnp.float32)
        update = (
            step_size
            / term_index
            * jnp.stack([own_part[0] + mirror_part[0], own_part[1] - mirror_part[1]])
        )
        summed = summed + update
        current = update.astype(jnp.bfloat16)
    result = jnp.where(upper_mask, summed[0], summed[1])
    return result[None]


MESH_ID = pl.DeviceIdType.MESH


def gather_kernel(
    sizes, packed_ref, h_real_ref, h_imag_ref, cols_ref, out_ref,
    whole, blocks, cols_vmem, cols_smem, current, generator,
    local_sem, send_sem, relay_sem, recv_sem, h_send, h_relay, h_recv, cols_send, cols_recv,
):
    bands, pieces, piece_len, block_len, local_blocks, slots = sizes
    rows_here = pieces * piece_len
    width = bands * piece_len
    order = bands * rows_here
    per_block = block_len // piece_len
    strip = 2 * piece_len
    z = lax.axis_index("row")
    x = lax.axis_index("col")
    s = lax.axis_index("sub")
    y = lax.axis_index("runs")
    piece = x * 2 + s
    x_peer, s_peer, y_peer = {"col": 1 - x}, {"sub": 1 - s}, {"runs": 1 - y}

    halves = 2
    half = pieces // halves

    def spot(band, owner, part):
        start = pl.multiple_of(owner * width, width)
        return whole.at[pl.ds(part * half, half), band, :, pl.ds(start, width)]

    def nearest(position):
        inner = jnp.minimum(z, bands - 1 - z)
        sign = 1 if position % 2 == 0 else -1
        beyond = jnp.where(z < bands - 1 - z, z + (position - inner), z - (position - inner))
        return jnp.where(position <= 2 * inner, z + sign * ((position + 1) // 2), beyond)

    others = [nearest(position) for position in range(1, bands)]
    loads = [
        pltpu.make_async_copy(
            packed_ref.at[pl.ds(part * half, half)], spot(z, piece, part), local_sem.at[part]
        )
        for part in range(halves)
    ]
    loads += [
        pltpu.make_async_copy(h_real_ref, blocks.at[0, z], local_sem.at[2]),
        pltpu.make_async_copy(h_imag_ref, blocks.at[1, z], local_sem.at[3]),
        pltpu.make_async_copy(cols_ref, cols_vmem.at[z], local_sem.at[4]),
    ]
    for load in loads:
        load.start()
    barrier = pltpu.get_barrier_semaphore()
    for step in range(1, bands):
        pl.semaphore_signal(
            barrier, 1, device_id={"row": lax.rem(z + step, bands)}, device_id_type=MESH_ID
        )
    for peer in (x_peer, s_peer, y_peer):
        pl.semaphore_signal(barrier, 1, device_id=peer, device_id_type=MESH_ID)
    pl.semaphore_wait(barrier, bands + 2)

    def send_packed(band, owner, part, sender, peer):
        return pltpu.make_async_remote_copy(
            src_ref=spot(band, owner, part), dst_ref=spot(band, owner, part), send_sem=sender,
            recv_sem=recv_sem.at[band, owner, part], device_id=peer, device_id_type=MESH_ID,
        )

    h_half = slots

    def send_h(kind, band, row, part, sender, peer):
        place = blocks.at[kind, band, row, pl.ds(part * h_half, h_half)]
        return pltpu.make_async_remote_copy(
            src_ref=place, dst_ref=place, send_sem=sender,
            recv_sem=h_recv.at[kind, band, row, part], device_id=peer, device_id_type=MESH_ID,
        )

    def send_cols(source, target):
        return pltpu.make_async_remote_copy(
            src_ref=cols_vmem.at[source], dst_ref=cols_vmem.at[source],
            send_sem=cols_send.at[target], recv_sem=cols_recv.at[source],
            device_id={"row": target}, device_id_type=MESH_ID,
        )

    up, down = {"row": lax.rem(z + 1, bands)}, {"row": lax.rem(z + bands - 1, bands)}
    has_up, has_down = z < bands - 1, z > 0

    def packed_up(band, part):
        return send_packed(band, piece, part, send_sem.at[0, band, part], up)

    def packed_down(band, part):
        return send_packed(band, piece, part, send_sem.at[1, band, part], down)

    def packed_side(band, part):
        return [send_packed(band, piece, part, send_sem.at[2, band, part], x_peer),
                send_packed(band, piece, part, send_sem.at[3, band, part], s_peer)]

    def packed_across(band, part):
        return send_packed(band, (1 - x) * 2 + s, part, relay_sem.at[band, part], s_peer)

    def h_up(band, part):
        return send_h(y, band, s, part, h_send.at[0, band, part], up)

    def h_down(band, part):
        return send_h(y, band, s, part, h_send.at[1, band, part], down)

    def h_side(band, part):
        return [send_h(y, band, s, part, h_send.at[2, band, part], y_peer),
                send_h(y, band, s, part, h_send.at[3, band, part], s_peer)]

    def h_across(band, part):
        return send_h(1 - y, band, s, part, h_relay.at[band, part], s_peer)

    def start_all(copies):
        for copy in copies:
            copy.start()

    def pass_on(copy):
        copy.wait_recv()
        copy.start()

    for part in range(halves):
        loads[part].wait()
        pl.when(has_up)(lambda: packed_up(z, part).start())
        pl.when(has_down)(lambda: packed_down(z, part).start())
        start_all(packed_side(z, part))
    for load in loads[halves:]:
        load.wait()
    for target in others:
        send_cols(z, target).start()
    pl.when(has_up)(lambda: h_up(z, 0).start())
    pl.when(has_down)(lambda: h_down(z, 0).start())

    def relay_step(step, make_up, make_down, make_side, count):
        below, above = z - step, z + step
        for part in range(count):
            @pl.when(below >= 0)
            def _():
                make_up(below, part).wait_recv()
                pl.when(has_up)(lambda: make_up(below, part).start())
                start_all(make_side(below, part))

            @pl.when(above < bands)
            def _():
                make_down(above, part).wait_recv()
                pl.when(has_down)(lambda: make_down(above, part).start())
                start_all(make_side(above, part))

    def cross_step(step, make_across, count):
        for part in range(count):
            pl.when(z - step >= 0)(lambda: pass_on(make_across(z - step, part)))
            pl.when(z + step < bands)(lambda: pass_on(make_across(z + step, part)))

    def h_ready(position):
        for kind in range(2):
            for part in range(1):
                send_h(
                    kind, others[position], 1 - s, part, h_relay.at[0, 0], s_peer
                ).wait_recv()

    for step in range(1, bands):
        relay_step(step, packed_up, packed_down, packed_side, halves)
        if step > 1:
            relay_step(step - 1, h_up, h_down, h_side, 1)
    for part in range(halves):
        pass_on(packed_across(z, part))
    for step in range(1, bands):
        cross_step(step, packed_across, halves)
    for step in range(1, bands - 2):
        cross_step(step, h_across, 1)
    for band in range(bands):
        for owner in (x * 2 + (1 - s), (1 - x) * 2 + (1 - s)):
            for part in range(halves):
                send_packed(band, owner, part, relay_sem.at[band, part], s_peer).wait_recv()

    def column_ids(count):
        place = lax.broadcasted_iota(jnp.int32, (1, count), 1)
        return place

    def natural(place):
        owner = place // width
        within = place - owner * width
        band = within // piece_len
        return band * rows_here + owner * piece_len + within - band * piece_len

    def turned(ref, start):
        tall = ref[:, :, :, pl.ds(start, strip)].reshape(order, strip)
        return jnp.transpose(tall)

    strips_per_piece = bands // 2

    def unpack(index, carry):
        start = pl.multiple_of(index * strip, strip)
        owner, band = index // strips_per_piece, index % strips_per_piece * 2
        here = whole[owner, pl.ds(band, 2)].reshape(strip, order)
        flipped = turned(whole, start)
        row_ids = natural(index * strip + lax.broadcasted_iota(jnp.int32, (strip, 1), 0))
        col_ids = natural(column_ids(order))
        here = here.astype(jnp.float32)
        flipped = flipped.astype(jnp.float32)
        gap = row_ids - col_ids
        real_part = jnp.where(gap <= 0, here, flipped)
        imag_part = jnp.where(gap > 0, here, jnp.where(gap < 0, -flipped, 0.0))
        shape = (2, piece_len, order)
        current[0, owner, pl.ds(band, 2)] = real_part.astype(jnp.bfloat16).reshape(shape)
        current[1, owner, pl.ds(band, 2)] = imag_part.astype(jnp.bfloat16).reshape(shape)
        return carry

    strips = pieces * strips_per_piece
    lax.fori_loop(0, strips // 2, unpack, 0)
    cross_step(bands - 2, h_across, 1)
    relay_step(bands - 1, h_up, h_down, h_side, 1)
    lax.fori_loop(strips // 2, strips, unpack, 0)
    for source in others:
        send_cols(source, source).wait_recv()
    to_smem = pltpu.make_async_copy(cols_vmem, cols_smem, local_sem.at[0])
    to_smem.start()
    to_smem.wait()
    cross_step(bands - 1, h_across, 1)

    def block_weights(band, row):
        real = jnp.concatenate([blocks[0, band, row, slot] for slot in range(slots)], axis=1)
        imag = jnp.concatenate([blocks[1, band, row, slot] for slot in range(slots)], axis=1)
        return jnp.concatenate(
            [jnp.concatenate([imag, real], axis=1), jnp.concatenate([-real, imag], axis=1)],
            axis=0,
        )

    def block_rows(band, row, start, count):
        found = []
        for part in range(2):
            for slot in range(slots):
                block = cols_smem[band, row, slot]
                for chunk in range(per_block):
                    place = block * per_block + chunk
                    found.append(
                        current[part, place % pieces, place // pieces, :, pl.ds(start, count)]
                    )
        return jnp.concatenate(found, axis=0)

    def multiply(block, start, count):
        band, row = block // local_blocks, block % local_blocks
        return jnp.dot(
            block_weights(band, row), block_rows(band, row, start, count),
            preferred_element_type=jnp.float32,
        ).astype(jnp.bfloat16)

    def generate(index, carry):
        block = index
        band, row = block // local_blocks, block % local_blocks
        weights = block_weights(band, row)
        span = width * 2
        for start in range(0, order, span):
            product = jnp.dot(
                weights, block_rows(band, row, start, span), preferred_element_type=jnp.float32
            ).astype(jnp.bfloat16)
            for part in range(2):
                for chunk in range(per_block):
                    place = block * per_block + chunk
                    first = part * block_len + chunk * piece_len
                    generator[part, place % pieces, place // pieces, :, pl.ds(start, span)] = (
                        product[first : first + piece_len]
                    )
        return carry

    def combine(factor):
        def body(index, carry):
            start = pl.multiple_of(index * strip, strip)
            owner, band = index // strips_per_piece, index % strips_per_piece * 2
            for part in range(2):
                own = generator[part, owner, pl.ds(band, 2)].reshape(strip, order)
                other = turned(generator.at[part], start)
                own = own.astype(jnp.float32)
                other = other.astype(jnp.float32)
                total = own + other if part == 0 else own - other
                current[part, owner, pl.ds(band, 2)] = (
                    (factor * total).astype(jnp.bfloat16).reshape(2, piece_len, order)
                )
            return carry

        return body

    mine = pl.ds(pl.multiple_of(piece * width, width), width)
    row_ids = z * rows_here + lax.broadcasted_iota(jnp.int32, (rows_here, 1), 0)
    col_place = lax.broadcasted_iota(jnp.int32, (1, width), 1)
    col_band = col_place // piece_len
    col_ids = col_band * rows_here + piece * piece_len + col_place - col_band * piece_len
    upper_mask = row_ids <= col_ids

    def own_rows(ref, part):
        return ref[part, :, z, :, mine].reshape(rows_here, width).astype(jnp.float32)

    def add_own(total):
        return total + jnp.where(upper_mask, own_rows(current, 0), own_rows(current, 1))

    out_ref[...] = jnp.where(upper_mask, own_rows(current, 0), own_rows(current, 1))
    blocks_total = bands * local_blocks
    for term in range(1, TERMS):
        if term == 1:
            lax.fori_loop(z * local_blocks, (z + 1) * local_blocks, generate, 0)
            for position, band in enumerate(others):
                h_ready(position)
                lax.fori_loop(band * local_blocks, (band + 1) * local_blocks, generate, 0)
        else:
            lax.fori_loop(0, blocks_total, generate, 0)
        lax.fori_loop(0, pieces * strips_per_piece, combine(step_size / term), 0)
        out_ref[...] = add_own(out_ref[...])

    for row in range(local_blocks):
        product = multiply(
            z * local_blocks + row, pl.multiple_of(piece * width, width), width
        )
        for part in range(2):
            for chunk in range(per_block):
                first = part * block_len + chunk * piece_len
                generator[part, row * per_block + chunk, z, :, mine] = (
                    product[first : first + piece_len]
                )
    own_real, own_imag = own_rows(generator, 0), own_rows(generator, 1)
    blocks_per_band = local_blocks

    def own_strip(owner):
        return pl.multiple_of(owner * width + z // 2 * strip, strip)

    def last_rows(index, carry):
        block = index * blocks_per_band + piece // per_block
        half = pl.multiple_of(piece % per_block * piece_len, piece_len)
        band, row = block // local_blocks, block % local_blocks
        rows = pl.ds(half, piece_len)
        real = jnp.concatenate([blocks[0, band, row, t, rows] for t in range(slots)], axis=1)
        imag = jnp.concatenate([blocks[1, band, row, t, rows] for t in range(slots)], axis=1)
        weights = jnp.concatenate(
            [jnp.concatenate([imag, real], axis=1), jnp.concatenate([-real, imag], axis=1)],
            axis=0,
        )
        for pair in range(0, pieces, 2):
            starts = [own_strip(owner) for owner in range(pair, pair + 2)]
            found = [block_rows(band, row, start, strip) for start in starts]
            product = jnp.dot(
                weights, jnp.concatenate(found, axis=1), preferred_element_type=jnp.float32
            ).astype(jnp.bfloat16)
            for side, start in enumerate(starts):
                for part in range(2):
                    generator[part, piece, index, :, pl.ds(start, strip)] = product[
                        part * piece_len : (part + 1) * piece_len,
                        side * strip : (side + 1) * strip,
                    ]
        return carry

    lax.fori_loop(0, bands, last_rows, 0)
    factor = step_size / TERMS
    for owner in range(pieces):
        first = own_strip(owner)
        for part in range(2):
            tall = generator[part, piece, :, :, pl.ds(first, strip)].reshape(width, strip)
            flat = jnp.transpose(tall).astype(jnp.float32)
            flat = jnp.where(z % 2 == 0, flat[:piece_len], flat[piece_len:])
            generator[part, owner, z, :, mine] = flat.astype(jnp.bfloat16)
    real_last = own_real + own_rows(generator, 0)
    imag_last = own_imag - own_rows(generator, 1)
    out_ref[...] = out_ref[...] + factor * jnp.where(upper_mask, real_last, imag_last)

    for part in range(halves):
        for copy in packed_side(z, part):
            copy.wait_send()
        pl.when(has_up)(lambda: packed_up(z, part).wait_send())
        pl.when(has_down)(lambda: packed_down(z, part).wait_send())
        packed_across(z, part).wait_send()
    pl.when(has_up)(lambda: h_up(z, 0).wait_send())
    pl.when(has_down)(lambda: h_down(z, 0).wait_send())
    for band in others:
        onward_up = jnp.logical_and(band < z, has_up)
        onward_down = jnp.logical_and(band > z, has_down)
        send_cols(z, band).wait_send()
        for copy in h_side(band, 0):
            copy.wait_send()
        h_across(band, 0).wait_send()
        pl.when(onward_up)(lambda: h_up(band, 0).wait_send())
        pl.when(onward_down)(lambda: h_down(band, 0).wait_send())
        for part in range(halves):
            for copy in packed_side(band, part):
                copy.wait_send()
            packed_across(band, part).wait_send()
            pl.when(onward_up)(lambda: packed_up(band, part).wait_send())
            pl.when(onward_down)(lambda: packed_down(band, part).wait_send())


def gathered_body(packed, h_real, h_imag, h_cols):
    bands, pieces = lax.axis_size("row"), lax.axis_size(("col", "sub"))
    rows_here, width = packed.shape[1], packed.shape[2]
    piece_len = rows_here // pieces
    local_blocks, slots, block_len, _ = h_real.shape
    order = bands * rows_here
    sizes = (bands, pieces, piece_len, block_len, local_blocks, slots)
    out = pl.pallas_call(
        functools.partial(gather_kernel, sizes),
        out_shape=jax.ShapeDtypeStruct((rows_here, width), jnp.float32),
        in_specs=[pl.BlockSpec(memory_space=pl.ANY)] * 4,
        out_specs=pl.BlockSpec(memory_space=pltpu.VMEM),
        scratch_shapes=[
            pltpu.VMEM((pieces, bands, piece_len, order), jnp.bfloat16),
            pltpu.VMEM((2, bands, local_blocks, slots, block_len, block_len), jnp.bfloat16),
            pltpu.VMEM((bands, local_blocks, slots), jnp.int32),
            pltpu.SMEM((bands, local_blocks, slots), jnp.int32),
            pltpu.VMEM((2, pieces, bands, piece_len, order), jnp.bfloat16),
            pltpu.VMEM((2, pieces, bands, piece_len, order), jnp.bfloat16),
            pltpu.SemaphoreType.DMA((5,)),
            pltpu.SemaphoreType.DMA((4, bands, 2)),
            pltpu.SemaphoreType.DMA((bands, 2)),
            pltpu.SemaphoreType.DMA((bands, pieces, 2)),
            pltpu.SemaphoreType.DMA((4, bands, 2)),
            pltpu.SemaphoreType.DMA((bands, 2)),
            pltpu.SemaphoreType.DMA((2, bands, local_blocks, 2)),
            pltpu.SemaphoreType.DMA((bands,)),
            pltpu.SemaphoreType.DMA((bands,)),
        ],
        compiler_params=pltpu.CompilerParams(collective_id=0, has_side_effects=True),
    )(packed.reshape(pieces, piece_len, width), h_real, h_imag, h_cols)
    return out[None]


def fits(mesh):
    def check(packed, h_real):
        shape = mesh.shape
        bands, pieces = shape["row"], shape["col"] * shape["sub"]
        rows_here = packed.shape[1] // (shape["runs"] * bands)
        piece_len = rows_here // pieces
        order = rows_here * bands
        held = 5 * 2 * order * order
        return (
            shape["col"] == 2 and shape["sub"] == 2 and shape["runs"] == 2
            and bands % 2 == 0 and packed.shape[2] == bands * piece_len
            and h_real.shape[0] == 2 * bands and h_real.shape[2] == 2 * piece_len
            and 2 * piece_len % 128 == 0 and held < 2**24
        )

    return check


def solution(mesh):
    in_specs = (
        P(("col", "sub"), ("runs", "row"), None),
        P("row", None, None, None),
        P("row", None, None, None),
        P("row", None),
    )
    out_specs = P(("col", "sub"), ("runs", "row"), None)

    def program(packed, h_real, h_imag, h_cols):
        chosen = gathered_body if fits(mesh)(packed, h_real) else body
        return jax.shard_map(
            chosen, mesh=mesh, in_specs=in_specs, out_specs=out_specs, check_vma=False
        )(packed, h_real, h_imag, h_cols)

    return program
```

profile of v0, /device:TPU:0, one launch (start us, length us, event | category | flops | bytes accessed | tf_op | source)
XLA Modules:
  0.0 54.1 jit_solution(9033472793960971385)
XLA Ops:
  0.0 52.4 %shard_map.46 = f32[256,256]{1,0:T(8,128)} custom-call(bf16[4,64,256]{2,1,0:T(8,128)(2,1)} %bitcast.3, bf16[2,4,128,128]{3,2,1,0:T(8,128)(2,1)} %h_real_ref.1, bf16[2,4,128,128]{3,2,1,0:T(8,128)(2,1)} %h_imag_ref.1, s32[2,4]{1,0:T(2,128)} %cols_ref.1), custom_call_target="tpu_custom_call" | custom-call | tf_op jit(solution)/shard_map/pallas_call | solution.py:486
  52.4 1.7 %copy.6 = f32[1,256,256]{2,1,0:T(8,128)} copy(f32[1,256,256]{2,1,0:T(8,128)} %bitcast.2) | data formatting | bytes 524288
where the time goes:
time: 54.2 us; the launch traced here: 54.1 us
  Pallas kernels  52.4 us (97%)
  local copies, waits for them, and re-layouts  1.67 us (3%)
    pallas_call x1, Pallas kernels, gathered_body(): pl.pallas_call(functools.partial(gather_kernel, sizes), out_shape=jax.Sha...  52.4 us
    unnamed x1, local copies, waits for them, and re-layouts  1.67 us

commit v1 on v0

--- a/solution.py
+++ b/solution.py
@@ -143,13 +143,18 @@
     for load in loads:
         load.start()
     barrier = pltpu.get_barrier_semaphore()
-    for step in range(1, bands):
-        pl.semaphore_signal(
-            barrier, 1, device_id={"row": lax.rem(z + step, bands)}, device_id_type=MESH_ID
-        )
-    for peer in (x_peer, s_peer, y_peer):
+    up, down = {"row": lax.rem(z + 1, bands)}, {"row": lax.rem(z + bands - 1, bands)}
+    has_up, has_down = z < bands - 1, z > 0
+
+    def greet(peer):
         pl.semaphore_signal(barrier, 1, device_id=peer, device_id_type=MESH_ID)
-    pl.semaphore_wait(barrier, bands + 2)
+
+    for peer in (s_peer, x_peer, y_peer):
+        greet(peer)
+    pl.when(has_up)(lambda: greet(up))
+    pl.when(has_down)(lambda: greet(down))
+    inside = jnp.logical_and(has_up, has_down)
+    pl.semaphore_wait(barrier, 3 + jnp.where(inside, 2, 1))
 
     def send_packed(band, owner, part, sender, peer):
         return pltpu.make_async_remote_copy(
@@ -166,15 +171,20 @@
             recv_sem=h_recv.at[kind, band, row, part], device_id=peer, device_id_type=MESH_ID,
         )
 
-    def send_cols(source, target):
+    def send_cols(band, sender, peer):
         return pltpu.make_async_remote_copy(
-            src_ref=cols_vmem.at[source], dst_ref=cols_vmem.at[source],
-            send_sem=cols_send.at[target], recv_sem=cols_recv.at[source],
-            device_id={"row": target}, device_id_type=MESH_ID,
-        )
-
-    up, down = {"row": lax.rem(z + 1, bands)}, {"row": lax.rem(z + bands - 1, bands)}
-    has_up, has_down = z < bands - 1, z > 0
+            src_ref=cols_vmem.at[band], dst_ref=cols_vmem.at[band], send_sem=sender,
+            recv_sem=cols_recv.at[band], device_id=peer, device_id_type=MESH_ID,
+        )
+
+    def cols_up(band, part):
+        return send_cols(band, cols_send.at[0, band], up)
+
+    def cols_down(band, part):
+        return send_cols(band, cols_send.at[1, band], down)
+
+    def no_side(band, part):
+        return []
 
     def packed_up(band, part):
         return send_packed(band, piece, part, send_sem.at[0, band, part], up)
@@ -217,8 +227,8 @@
         start_all(packed_side(z, part))
     for load in loads[halves:]:
         load.wait()
-    for target in others:
-        send_cols(z, target).start()
+    pl.when(has_up)(lambda: cols_up(z, 0).start())
+    pl.when(has_down)(lambda: cols_down(z, 0).start())
     pl.when(has_up)(lambda: h_up(z, 0).start())
     pl.when(has_down)(lambda: h_down(z, 0).start())
 
@@ -251,14 +261,19 @@
 
     for step in range(1, bands):
         relay_step(step, packed_up, packed_down, packed_side, halves)
-        if step > 1:
+        if step == 1:
+            for part in range(halves):
+                pass_on(packed_across(z, part))
+        else:
+            cross_step(step - 1, packed_across, halves)
+            relay_step(step - 1, cols_up, cols_down, no_side, 1)
+        if step == 2:
             relay_step(step - 1, h_up, h_down, h_side, 1)
-    for part in range(halves):
-        pass_on(packed_across(z, part))
-    for step in range(1, bands):
-        cross_step(step, packed_across, halves)
-    for step in range(1, bands - 2):
-        cross_step(step, h_across, 1)
+    cross_step(bands - 1, packed_across, halves)
+    relay_step(bands - 1, cols_up, cols_down, no_side, 1)
+    cross_step(1, h_across, 1)
+    for step in range(2, bands - 1):
+        relay_step(step, h_up, h_down, h_side, 1)
     for band in range(bands):
         for owner in (x * 2 + (1 - s), (1 - x) * 2 + (1 - s)):
             for part in range(halves):
@@ -299,15 +314,13 @@
 
     strips = pieces * strips_per_piece
     lax.fori_loop(0, strips // 2, unpack, 0)
-    cross_step(bands - 2, h_across, 1)
     relay_step(bands - 1, h_up, h_down, h_side, 1)
     lax.fori_loop(strips // 2, strips, unpack, 0)
-    for source in others:
-        send_cols(source, source).wait_recv()
+    for step in range(2, bands - 1):
+        cross_step(step, h_across, 1)
     to_smem = pltpu.make_async_copy(cols_vmem, cols_smem, local_sem.at[0])
     to_smem.start()
     to_smem.wait()
-    cross_step(bands - 1, h_across, 1)
 
     def block_weights(band, row):
         real = jnp.concatenate([blocks[0, band, row, slot] for slot in range(slots)], axis=1)
@@ -390,6 +403,8 @@
         if term == 1:
             lax.fori_loop(z * local_blocks, (z + 1) * local_blocks, generate, 0)
             for position, band in enumerate(others):
+                if position == len(others) - 2:
+                    cross_step(bands - 1, h_across, 1)
                 h_ready(position)
                 lax.fori_loop(band * local_blocks, (band + 1) * local_blocks, generate, 0)
         else:
@@ -459,10 +474,13 @@
         packed_across(z, part).wait_send()
     pl.when(has_up)(lambda: h_up(z, 0).wait_send())
     pl.when(has_down)(lambda: h_down(z, 0).wait_send())
+    pl.when(has_up)(lambda: cols_up(z, 0).wait_send())
+    pl.when(has_down)(lambda: cols_down(z, 0).wait_send())
     for band in others:
         onward_up = jnp.logical_and(band < z, has_up)
         onward_down = jnp.logical_and(band > z, has_down)
-        send_cols(z, band).wait_send()
+        pl.when(onward_up)(lambda: cols_up(band, 0).wait_send())
+        pl.when(onward_down)(lambda: cols_down(band, 0).wait_send())
         for copy in h_side(band, 0):
             copy.wait_send()
         h_across(band, 0).wait_send()
@@ -502,7 +520,7 @@
             pltpu.SemaphoreType.DMA((4, bands, 2)),
             pltpu.SemaphoreType.DMA((bands, 2)),
             pltpu.SemaphoreType.DMA((2, bands, local_blocks, 2)),
-            pltpu.SemaphoreType.DMA((bands,)),
+            pltpu.SemaphoreType.DMA((2, bands)),
             pltpu.SemaphoreType.DMA((bands,)),
         ],
         compiler_params=pltpu.CompilerParams(collective_id=0, has_side_effects=True),
@@ -520,7 +538,7 @@
         held = 5 * 2 * order * order
         return (
             shape["col"] == 2 and shape["sub"] == 2 and shape["runs"] == 2
-            and bands % 2 == 0 and packed.shape[2] == bands * piece_len
+            and bands % 2 == 0 and bands > 2 and packed.shape[2] == bands * piece_len
             and h_real.shape[0] == 2 * bands and h_real.shape[2] == 2 * piece_len
             and 2 * piece_len % 128 == 0 and held < 2**24
         )

time: 54.2 us -> 51.1 us (0.943)
  Pallas kernels: 52.4 us -> 49.3 us
    pallas_call x1, Pallas kernels: 52.4 us -> 49.3 us  [gathered_body(): pl.pallas_call(functools.partial(gather_kernel, sizes), out_shape=jax.Sha...]
where the time goes in v1:
time: 51.1 us; the launch traced here: 50.9 us
  Pallas kernels  49.3 us (96%)
  local copies, waits for them, and re-layouts  1.67 us (3%)
    pallas_call x1, Pallas kernels, gathered_body(): pl.pallas_call(functools.partial(gather_kernel, sizes), out_shape=jax.Sha...  49.3 us
    unnamed x1, local copies, waits for them, and re-layouts  1.67 us

profile of v1, /device:TPU:0, one launch (start us, length us, event | category | flops | bytes accessed | tf_op | source)
XLA Modules:
  0.0 50.9 jit_solution(17803324294096711296)
XLA Ops:
  0.0 49.3 %shard_map.46 = f32[256,256]{1,0:T(8,128)} custom-call(bf16[4,64,256]{2,1,0:T(8,128)(2,1)} %bitcast.3, bf16[2,4,128,128]{3,2,1,0:T(8,128)(2,1)} %h_real_ref.1, bf16[2,4,128,128]{3,2,1,0:T(8,128)(2,1)} %h_imag_ref.1, s32[2,4]{1,0:T(2,128)} %cols_ref.1), custom_call_target="tpu_custom_call" | custom-call | tf_op jit(solution)/shard_map/pallas_call | solution.py:504
  49.3 1.7 %copy.6 = f32[1,256,256]{2,1,0:T(8,128)} copy(f32[1,256,256]{2,1,0:T(8,128)} %bitcast.2) | data formatting | bytes 524288

commit v2 on v1

--- a/solution.py
+++ b/solution.py
@@ -99,7 +99,7 @@
 
 def gather_kernel(
     sizes, packed_ref, h_real_ref, h_imag_ref, cols_ref, out_ref,
-    whole, blocks, cols_vmem, cols_smem, current, generator,
+    whole, blocks, cols_vmem, cols_smem, current, generator, kept_weights, identity,
     local_sem, send_sem, relay_sem, recv_sem, h_send, h_relay, h_recv, cols_send, cols_recv,
 ):
     bands, pieces, piece_len, block_len, local_blocks, slots = sizes
@@ -142,6 +142,10 @@
     ]
     for load in loads:
         load.start()
+    identity[...] = jnp.where(
+        lax.broadcasted_iota(jnp.int32, (width, width), 0)
+        == lax.broadcasted_iota(jnp.int32, (width, width), 1), 1.0, 0.0,
+    ).astype(jnp.bfloat16)
     barrier = pltpu.get_barrier_semaphore()
     up, down = {"row": lax.rem(z + 1, bands)}, {"row": lax.rem(z + bands - 1, bands)}
     has_up, has_down = z < bands - 1, z > 0
@@ -229,8 +233,16 @@
         load.wait()
     pl.when(has_up)(lambda: cols_up(z, 0).start())
     pl.when(has_down)(lambda: cols_down(z, 0).start())
-    pl.when(has_up)(lambda: h_up(z, 0).start())
-    pl.when(has_down)(lambda: h_down(z, 0).start())
+
+    def begin_h(step):
+        up_at = jnp.where(z == bands - 2, 0, z)
+        down_at = jnp.where(z == 1, 0, bands - 1 - z)
+        now_up = jnp.logical_and(up_at == step, has_up)
+        now_down = jnp.logical_and(down_at == step, has_down)
+        pl.when(now_up)(lambda: h_up(z, 0).start())
+        pl.when(now_down)(lambda: h_down(z, 0).start())
+
+    begin_h(0)
 
     def relay_step(step, make_up, make_down, make_side, count):
         below, above = z - step, z + step
@@ -259,69 +271,102 @@
                     kind, others[position], 1 - s, part, h_relay.at[0, 0], s_peer
                 ).wait_recv()
 
-    for step in range(1, bands):
-        relay_step(step, packed_up, packed_down, packed_side, halves)
-        if step == 1:
-            for part in range(halves):
-                pass_on(packed_across(z, part))
-        else:
-            cross_step(step - 1, packed_across, halves)
-            relay_step(step - 1, cols_up, cols_down, no_side, 1)
-        if step == 2:
-            relay_step(step - 1, h_up, h_down, h_side, 1)
-    cross_step(bands - 1, packed_across, halves)
-    relay_step(bands - 1, cols_up, cols_down, no_side, 1)
-    cross_step(1, h_across, 1)
-    for step in range(2, bands - 1):
-        relay_step(step, h_up, h_down, h_side, 1)
-    for band in range(bands):
+    pairs = bands // 2
+    own_pair = z // 2
+
+    def within_pair(place):
+        return place // piece_len * rows_here + place % piece_len
+
+    base_gap = within_pair(lax.broadcasted_iota(jnp.int32, (strip, 1), 0)) - within_pair(
+        lax.broadcasted_iota(jnp.int32, (1, strip), 1)
+    )
+
+    def strip_at(owner, pair):
+        return pl.multiple_of(owner * width + pair * strip, strip)
+
+    def tile(ref, owner, pair, start):
+        return ref[owner, pl.ds(pair * 2, 2), :, pl.ds(start, strip)].reshape(strip, strip)
+
+    def place_tile(part, owner, pair, start, value):
+        current[part, owner, pl.ds(pair * 2, 2), :, pl.ds(start, strip)] = (
+            value.astype(jnp.bfloat16).reshape(2, piece_len, strip)
+        )
+
+    def unpack_same(pair):
+        def body(owner, carry):
+            start = strip_at(owner, pair)
+            for other in range(pieces):
+                there = strip_at(other, pair)
+                here = tile(whole, owner, pair, there).astype(jnp.float32)
+                flipped = jnp.transpose(tile(whole, other, pair, start)).astype(jnp.float32)
+                gap = base_gap + (owner - other) * piece_len
+                place_tile(0, owner, pair, there, jnp.where(gap <= 0, here, flipped))
+                place_tile(
+                    1, owner, pair, there,
+                    jnp.where(gap > 0, here, jnp.where(gap < 0, -flipped, 0.0)),
+                )
+            return carry
+
+        lax.fori_loop(0, pieces, body, 0)
+
+    def unpack_apart(low, high):
+        def body(owner, carry):
+            start = strip_at(owner, low)
+            for other in range(pieces):
+                there = strip_at(other, high)
+                upper = tile(whole, owner, low, there)
+                lower = tile(whole, other, high, start)
+                place_tile(0, owner, low, there, upper)
+                place_tile(1, other, high, start, lower)
+                place_tile(0, other, high, start, jnp.transpose(upper))
+                place_tile(1, owner, low, there, -jnp.transpose(lower))
+            return carry
+
+        lax.fori_loop(0, pieces, body, 0)
+
+    def packed_ready(band):
         for owner in (x * 2 + (1 - s), (1 - x) * 2 + (1 - s)):
             for part in range(halves):
                 send_packed(band, owner, part, relay_sem.at[band, part], s_peer).wait_recv()
 
-    def column_ids(count):
-        place = lax.broadcasted_iota(jnp.int32, (1, count), 1)
-        return place
-
-    def natural(place):
-        owner = place // width
-        within = place - owner * width
-        band = within // piece_len
-        return band * rows_here + owner * piece_len + within - band * piece_len
-
-    def turned(ref, start):
-        tall = ref[:, :, :, pl.ds(start, strip)].reshape(order, strip)
-        return jnp.transpose(tall)
-
-    strips_per_piece = bands // 2
-
-    def unpack(index, carry):
-        start = pl.multiple_of(index * strip, strip)
-        owner, band = index // strips_per_piece, index % strips_per_piece * 2
-        here = whole[owner, pl.ds(band, 2)].reshape(strip, order)
-        flipped = turned(whole, start)
-        row_ids = natural(index * strip + lax.broadcasted_iota(jnp.int32, (strip, 1), 0))
-        col_ids = natural(column_ids(order))
-        here = here.astype(jnp.float32)
-        flipped = flipped.astype(jnp.float32)
-        gap = row_ids - col_ids
-        real_part = jnp.where(gap <= 0, here, flipped)
-        imag_part = jnp.where(gap > 0, here, jnp.where(gap < 0, -flipped, 0.0))
-        shape = (2, piece_len, order)
-        current[0, owner, pl.ds(band, 2)] = real_part.astype(jnp.bfloat16).reshape(shape)
-        current[1, owner, pl.ds(band, 2)] = imag_part.astype(jnp.bfloat16).reshape(shape)
-        return carry
-
-    strips = pieces * strips_per_piece
-    lax.fori_loop(0, strips // 2, unpack, 0)
-    relay_step(bands - 1, h_up, h_down, h_side, 1)
-    lax.fori_loop(strips // 2, strips, unpack, 0)
+    outside = jnp.logical_not(inside)
+    relay_step(1, packed_up, packed_down, packed_side, halves)
+    begin_h(1)
+    for part in range(halves):
+        pass_on(packed_across(z, part))
+    pl.when(outside)(lambda: relay_step(1, h_up, h_down, h_side, 1))
+    relay_step(2, packed_up, packed_down, packed_side, halves)
+    begin_h(2)
+    cross_step(1, packed_across, halves)
+    relay_step(1, cols_up, cols_down, no_side, 1)
+    pl.when(inside)(lambda: relay_step(1, h_up, h_down, h_side, 1))
+    for step in range(3, bands):
+        relay_step(step, packed_up, packed_down, packed_side, halves)
+        begin_h(step)
     for step in range(2, bands - 1):
-        cross_step(step, h_across, 1)
+        cross_step(step, packed_across, halves)
+        relay_step(step, cols_up, cols_down, no_side, 1)
+    packed_ready(own_pair * 2)
+    packed_ready(own_pair * 2 + 1)
+    unpack_same(own_pair)
+    cross_step(bands - 1, packed_across, halves)
+    relay_step(bands - 1, cols_up, cols_down, no_side, 1)
     to_smem = pltpu.make_async_copy(cols_vmem, cols_smem, local_sem.at[0])
     to_smem.start()
+    for step in range(2, bands - 1):
+        relay_step(step, h_up, h_down, h_side, 1)
+    cross_step(1, h_across, 1)
+    for step in range(1, pairs):
+        later = lax.rem(own_pair + step, pairs)
+        packed_ready(later * 2)
+        packed_ready(later * 2 + 1)
+    for low in range(pairs):
+        for high in range(low + 1, pairs):
+            unpack_apart(low, high)
+    relay_step(bands - 1, h_up, h_down, h_side, 1)
+    for step in range(1, pairs):
+        unpack_same(lax.rem(own_pair + step, pairs))
     to_smem.wait()
-
     def block_weights(band, row):
         real = jnp.concatenate([blocks[0, band, row, slot] for slot in range(slots)], axis=1)
         imag = jnp.concatenate([blocks[1, band, row, slot] for slot in range(slots)], axis=1)
@@ -349,42 +394,49 @@
             preferred_element_type=jnp.float32,
         ).astype(jnp.bfloat16)
 
-    def generate(index, carry):
-        block = index
-        band, row = block // local_blocks, block % local_blocks
-        weights = block_weights(band, row)
-        span = width * 2
-        for start in range(0, order, span):
-            product = jnp.dot(
-                weights, block_rows(band, row, start, span), preferred_element_type=jnp.float32
-            ).astype(jnp.bfloat16)
+    span = order // 2
+
+    def generate(term, band):
+        for row in range(local_blocks):
+            if term == 1:
+                kept_weights[band, row] = block_weights(band, row)
+            for start in range(0, order, span):
+                product = jnp.dot(
+                    kept_weights[band, row], block_rows(band, row, start, span),
+                    preferred_element_type=jnp.float32,
+                ).astype(jnp.bfloat16)
+                for part in range(2):
+                    for chunk in range(per_block):
+                        first = part * block_len + chunk * piece_len
+                        generator[part, row * per_block + chunk, band, :, pl.ds(start, span)] = (
+                            product[first : first + piece_len]
+                        )
+
+    mine = pl.ds(pl.multiple_of(piece * width, width), width)
+
+    def flip(tall):
+        return lax.dot_general(
+            identity[...], tall, (((1,), (1,)), ((), ())), preferred_element_type=jnp.float32
+        )
+
+    def joined(own, tall, part, factor):
+        mirrored = flip(tall)
+        own = own.astype(jnp.float32)
+        total = own + mirrored if part == 0 else own - mirrored
+        return (factor * total).astype(jnp.bfloat16)
+
+    def combine_all(factor):
+        def body(owner, carry):
+            lanes = pl.ds(pl.multiple_of(owner * width, width), width)
             for part in range(2):
-                for chunk in range(per_block):
-                    place = block * per_block + chunk
-                    first = part * block_len + chunk * piece_len
-                    generator[part, place % pieces, place // pieces, :, pl.ds(start, span)] = (
-                        product[first : first + piece_len]
-                    )
-        return carry
-
-    def combine(factor):
-        def body(index, carry):
-            start = pl.multiple_of(index * strip, strip)
-            owner, band = index // strips_per_piece, index % strips_per_piece * 2
-            for part in range(2):
-                own = generator[part, owner, pl.ds(band, 2)].reshape(strip, order)
-                other = turned(generator.at[part], start)
-                own = own.astype(jnp.float32)
-                other = other.astype(jnp.float32)
-                total = own + other if part == 0 else own - other
-                current[part, owner, pl.ds(band, 2)] = (
-                    (factor * total).astype(jnp.bfloat16).reshape(2, piece_len, order)
-                )
+                own = generator[part, owner].reshape(width, order)
+                tall = generator[part, :, :, :, lanes].reshape(order, width)
+                total = joined(own, tall, part, factor)
+                current[part, owner] = total.reshape(bands, piece_len, order)
             return carry
 
-        return body
-
-    mine = pl.ds(pl.multiple_of(piece * width, width), width)
+        lax.fori_loop(0, pieces, body, 0, unroll=True)
+
     row_ids = z * rows_here + lax.broadcasted_iota(jnp.int32, (rows_here, 1), 0)
     col_place = lax.broadcasted_iota(jnp.int32, (1, width), 1)
     col_band = col_place // piece_len
@@ -398,20 +450,16 @@
         return total + jnp.where(upper_mask, own_rows(current, 0), own_rows(current, 1))
 
     out_ref[...] = jnp.where(upper_mask, own_rows(current, 0), own_rows(current, 1))
-    blocks_total = bands * local_blocks
     for term in range(1, TERMS):
-        if term == 1:
-            lax.fori_loop(z * local_blocks, (z + 1) * local_blocks, generate, 0)
-            for position, band in enumerate(others):
-                if position == len(others) - 2:
-                    cross_step(bands - 1, h_across, 1)
+        generate(term, z)
+        for position, band in enumerate(others):
+            if term == 1:
+                if position < bands - 2:
+                    cross_step(position + 2, h_across, 1)
                 h_ready(position)
-                lax.fori_loop(band * local_blocks, (band + 1) * local_blocks, generate, 0)
-        else:
-            lax.fori_loop(0, blocks_total, generate, 0)
-        lax.fori_loop(0, pieces * strips_per_piece, combine(step_size / term), 0)
+            generate(term, band)
+        combine_all(step_size / term)
         out_ref[...] = add_own(out_ref[...])
-
     for row in range(local_blocks):
         product = multiply(
             z * local_blocks + row, pl.multiple_of(piece * width, width), width
@@ -423,37 +471,26 @@
                     product[first : first + piece_len]
                 )
     own_real, own_imag = own_rows(generator, 0), own_rows(generator, 1)
-    blocks_per_band = local_blocks
 
     def own_strip(owner):
-        return pl.multiple_of(owner * width + z // 2 * strip, strip)
-
-    def last_rows(index, carry):
-        block = index * blocks_per_band + piece // per_block
-        half = pl.multiple_of(piece % per_block * piece_len, piece_len)
-        band, row = block // local_blocks, block % local_blocks
-        rows = pl.ds(half, piece_len)
-        real = jnp.concatenate([blocks[0, band, row, t, rows] for t in range(slots)], axis=1)
-        imag = jnp.concatenate([blocks[1, band, row, t, rows] for t in range(slots)], axis=1)
+        return strip_at(owner, own_pair)
+
+    row = piece // per_block
+    offset = pl.multiple_of(piece % per_block * piece_len, piece_len)
+    for band in range(bands):
         weights = jnp.concatenate(
-            [jnp.concatenate([imag, real], axis=1), jnp.concatenate([-real, imag], axis=1)],
+            [kept_weights[band, row, pl.ds(part * block_len + offset, piece_len)] for part in range(2)],
             axis=0,
         )
-        for pair in range(0, pieces, 2):
-            starts = [own_strip(owner) for owner in range(pair, pair + 2)]
-            found = [block_rows(band, row, start, strip) for start in starts]
-            product = jnp.dot(
-                weights, jnp.concatenate(found, axis=1), preferred_element_type=jnp.float32
-            ).astype(jnp.bfloat16)
-            for side, start in enumerate(starts):
-                for part in range(2):
-                    generator[part, piece, index, :, pl.ds(start, strip)] = product[
-                        part * piece_len : (part + 1) * piece_len,
-                        side * strip : (side + 1) * strip,
-                    ]
-        return carry
-
-    lax.fori_loop(0, bands, last_rows, 0)
+        found = [block_rows(band, row, own_strip(owner), strip) for owner in range(pieces)]
+        product = jnp.dot(
+            weights, jnp.concatenate(found, axis=1), preferred_element_type=jnp.float32
+        ).astype(jnp.bfloat16)
+        for owner in range(pieces):
+            for part in range(2):
+                generator[part, piece, band, :, pl.ds(own_strip(owner), strip)] = product[
+                    part * piece_len : (part + 1) * piece_len, owner * strip : (owner + 1) * strip
+                ]
     factor = step_size / TERMS
     for owner in range(pieces):
         first = own_strip(owner)
@@ -513,6 +550,10 @@
             pltpu.SMEM((bands, local_blocks, slots), jnp.int32),
             pltpu.VMEM((2, pieces, bands, piece_len, order), jnp.bfloat16),
             pltpu.VMEM((2, pieces, bands, piece_len, order), jnp.bfloat16),
+            pltpu.VMEM(
+                (bands, local_blocks, 2 * block_len, 2 * slots * block_len), jnp.bfloat16
+            ),
+            pltpu.VMEM((width, width), jnp.bfloat16),
             pltpu.SemaphoreType.DMA((5,)),
             pltpu.SemaphoreType.DMA((4, bands, 2)),
             pltpu.SemaphoreType.DMA((bands, 2)),

time: 51.1 us -> 44.6 us (0.87)
  Pallas kernels: 49.3 us -> 42.8 us
    pallas_call x1, Pallas kernels: 49.3 us -> 42.8 us  [gathered_body(): pl.pallas_call(functools.partial(gather_kernel, sizes), out_shape=jax.Sha...]
where the time goes in v2:
time: 44.6 us; the launch traced here: 44.5 us
  Pallas kernels  42.8 us (96%)
  local copies, waits for them, and re-layouts  1.67 us (4%)
    pallas_call x1, Pallas kernels, gathered_body(): pl.pallas_call(functools.partial(gather_kernel, sizes), out_shape=jax.Sha...  42.8 us
    unnamed x1, local copies, waits for them, and re-layouts  1.67 us

profile of v2, /device:TPU:0, one launch (start us, length us, event | category | flops | bytes accessed | tf_op | source)
XLA Modules:
  0.0 44.5 jit_solution(15558851982892355771)
XLA Ops:
  0.0 42.8 %shard_map.46 = f32[256,256]{1,0:T(8,128)} custom-call(bf16[4,64,256]{2,1,0:T(8,128)(2,1)} %bitcast.3, bf16[2,4,128,128]{3,2,1,0:T(8,128)(2,1)} %h_real_ref.1, bf16[2,4,128,128]{3,2,1,0:T(8,128)(2,1)} %h_imag_ref.1, s32[2,4]{1,0:T(2,128)} %cols_ref.1), custom_call_target="tpu_custom_call" | custom-call | tf_op jit(solution)/shard_map/pallas_call | solution.py:541
  42.8 1.7 %copy.6 = f32[1,256,256]{2,1,0:T(8,128)} copy(f32[1,256,256]{2,1,0:T(8,128)} %bitcast.2) | data formatting | bytes 524288
